TPU v7x, 512 devices: a whole 4x4x16 slice. The times are simulated.
512 devices in a mesh: modes: 64 (over z_lo, x, core), rad: 8 (over z_hi, y).
Axes of the slice: x: 4, y: 4, z: 16 (z_hi: 2, z_lo: 8; z = z_hi * 8 + z_lo), core: 2. Of those that a mesh axis runs over, the one named last changes fastest.
Arguments:
- forcing: bfloat16 [3, 1024, 256, 256], P(None, 'modes', 'rad'), may hold values from -6 to 6
- diffusion: float32 [3], replicated, may hold values from 0.05 to 1
- axial_forward: float32 [256, 256], replicated, may hold values from -0.375 to 0.375
- axial_inverse_map: float32 [256, 256], replicated, may hold values from -0.375 to 0.375
- axial_eigenvalues: float32 [256], replicated, may hold values from 0.05 to 10
- radial_forward: float32 [512, 256, 256], P(('modes', 'rad')), may hold values from -0.375 to 0.375
- radial_backward: float32 [512, 256, 256], P(('modes', 'rad')), may hold values from -0.375 to 0.375
- radial_eigenvalues: float32 [512, 256], P(('modes', 'rad')), may hold values from 0.05 to 10
Outputs:
- solution: float32 [3, 512, 2, 256, 256], P(None, 'modes', None, 'rad')
All inputs are finite; a program needn't handle non-finite values.
Results may differ from a plain program's by a relative error of at most 0.0003.
Values may be sent and summed in bfloat16 or wider, within the bound.
A program may use at most 64 MiB of HBM per device.

v0:
```python
import math
import jax
import jax.numpy as jnp
from jax import lax
from jax.sharding import PartitionSpec as P

GLOBAL = True


def split_table(points, rows):
    k = jnp.arange(rows, dtype=jnp.int32)
    t = jnp.arange(points, dtype=jnp.int32)
    quarter = (k % 2).astype(jnp.float32) * (0.5 * math.pi)
    phase = (k // 2)[:, None] * t[None, :] % points
    radians = phase.astype(jnp.float32) * (2.0 * math.pi / points) + quarter[:, None]
    table = jnp.cos(radians) * (1.0 / math.sqrt(points))
    upper = table.astype(jnp.bfloat16)
    widened = lax.optimization_barrier(upper).astype(jnp.float32)
    lower = (table - widened).astype(jnp.bfloat16)
    return (upper, lower)


def per_device(
    forcing,
    diffusion,
    axial_forward,
    axial_inverse_map,
    axial_eigenvalues,
    radial_forward,
    radial_backward,
    radial_eigenvalues,
):
    hi = lax.Precision.HIGHEST
    fields, slab, rblock, nz = forcing.shape
    nm, nrad = (lax.axis_size("modes"), lax.axis_size("rad"))
    points = slab * nm
    nr = rblock * nrad
    modes = nm * nrad
    cols = rblock * nz // nm
    halves = nz // cols
    up, lo = split_table(points, 2 * modes)
    x = forcing.reshape(fields, slab, rblock, halves, cols)
    x = x.transpose(2, 3, 0, 1, 4).reshape(nm, fields, slab, cols)
    got = lax.all_to_all(x, "modes", split_axis=0, concat_axis=0, tiled=True)
    got = got.transpose(0, 2, 1, 3).reshape(points, fields * cols)
    spec = jnp.dot(up, got, preferred_element_type=jnp.float32) + jnp.dot(
        lo, got, preferred_element_type=jnp.float32
    )
    if GLOBAL:
        spec = spec.reshape(modes, 2, fields * cols)
        here = lax.all_to_all(spec, ("modes", "rad"), split_axis=0, concat_axis=0, tiled=True)
        here = here.reshape(nm, nrad, 2, fields, cols)
    else:
        spec = spec.reshape(nm, nrad, 2, fields * cols)
        here = lax.all_to_all(spec, "modes", split_axis=0, concat_axis=0, tiled=True)
        here = lax.all_to_all(here, "rad", split_axis=1, concat_axis=1, tiled=True)
        here = here.reshape(nm, nrad, 2, fields, cols)
    here = here.reshape(rblock, halves, nrad, 2, fields, cols)
    here = here.transpose(4, 3, 2, 0, 1, 5).reshape(fields, 2, nr, nz)
    axial = jnp.einsum("fcrz,qz->fcrq", here, axial_forward, precision=hi)
    radial = jnp.einsum("ir,fcrq->fciq", radial_forward[0], axial, precision=hi)
    denominator = 1.0 + diffusion[:, None, None, None] * (
        radial_eigenvalues[0][None, None, :, None] + axial_eigenvalues[None, None, None, :]
    )
    scaled = radial / denominator
    returned = jnp.einsum("ri,fciq->fcrq", radial_backward[0], scaled, precision=hi)
    out = jnp.einsum("zq,fcrq->fcrz", axial_inverse_map, returned, precision=hi)
    out = out.reshape(fields, 1, 2, nr, nz)
    return lax.all_to_all(out, "rad", split_axis=3, concat_axis=1, tiled=True)


def solution(mesh):
    in_specs = (
        P(None, "modes", "rad", None),
        P(),
        P(),
        P(),
        P(),
        P(("modes", "rad"), None, None),
        P(("modes", "rad"), None, None),
        P(("modes", "rad"), None),
    )
    return jax.shard_map(
        per_device,
        mesh=mesh,
        in_specs=in_specs,
        out_specs=P(None, "modes", None, "rad", None),
        check_vma=False,
    )
```

profile of v0, /device:TPU:32, one launch (start us, length us, event | category | flops | bytes accessed | tf_op | source)
XLA Modules:
  0.0 291.1 jit_solution(4464815962577270002)
XLA Ops:
  0.0 0.0 copy-start
  0.0 2.1 reshape.85
  2.1 1.8 copy.14
  3.9 15.7 %all-to-all-start = ((bf16[64,3,16,128]{3,2,1,0:T(8,128)(2,1)}), bf16[64,3,16,128]{3,2,1,0:T(8,128)(2,1)S(1)}, u32[]{:S(2)}, u32[]{:S(2)}) async-start(bf16[64,3,16,128]{3,2,1,0:T(8,128)(2,1)} %bitcast.1), calls=%async_computation | async-start | bytes 1572864 | tf_op jit(solution)/shard_map/all_to_all | solution.py:44
  19.5 17.6 %fusion.11 = bf16[1024,1024]{1,0:T(8,128)(2,1)S(1)} fusion(f32[1024]{0:T(1024)S(1)} %fusion.37, s32[1024]{0:T(1024)S(1)} %add_select_fusion.1), kind=kLoop, calls=%fused_computation.14 | loop fusion | flops 17825792 | bytes 2105344 | tf_op jit(solution)/shard_map/convert_element_type | solution.py:17
  37.1 20.4 %all-to-all-done = bf16[64,3,16,128]{3,2,1,0:T(8,128)(2,1)S(1)} async-done(((bf16[64,3,16,128]{3,2,1,0:T(8,128)(2,1)}), bf16[64,3,16,128]{3,2,1,0:T(8,128)(2,1)S(1)}, u32[]{:S(2)}, u32[]{:S(2)}) %all-to-all-start) | async-done | bytes 786464 | tf_op jit(solution)/shard_map/all_to_all | solution.py:44
  57.5 0.5 copy.15
  58.0 16.7 %fusion.9 = f32[1024,384]{1,0:T(8,128)S(1)} fusion(bf16[1024,1024]{1,0:T(8,128)(2,1)S(1)} %fusion.11, f32[1024]{0:T(1024)S(1)} %fusion.37, s32[1024]{0:T(1024)S(1)} %add_select_fusion.1, bf16[128,8,3,128]{3,2,1,0:T(4,128)(2,1)S(1)} %bitcast.62), kind=kOutput, calls=%fused_computation.13 | convolution fusion | flops 825229312 | bytes 4464640 | tf_op jit(solution)/shard_map/dot_general | solution.py:46
  74.8 16.4 %convolution_add_fusion = f32[1024,384]{1,0:T(8,128)S(1)} fusion(f32[1024,384]{1,0:T(8,128)S(1)} %fusion.9, bf16[128,8,3,128]{3,2,1,0:T(4,128)(2,1)S(1)} %bitcast.63, f32[1024]{0:T(1024)S(1)} %fusion.37, s32[1024]{0:T(1024)S(1)} %add_select_fusion.1), kind=kOutput, calls=%fused_computation.21 | convolution fusion | flops 823525376 | bytes 3940352 | tf_op jit(solution)/shard_map/dot_general | solution.py:46
  91.1 2.1 reshape.88
  93.2 18.3 %all-to-all-start.1 = ((f32[512,2,384]{2,1,0:T(2,128)}), f32[512,2,384]{2,1,0:T(2,128)S(1)}, u32[]{:S(2)}, u32[]{:S(2)}) async-start(f32[512,2,384]{2,1,0:T(2,128)} %reshape.88), calls=%async_computation.1 | async-start | bytes 3145728 | tf_op jit(solution)/shard_map/all_to_all | solution.py:51
  111.5 0.0 copy-done.3
  111.5 0.0 copy-done.4
  111.6 0.1 broadcast_add_fusion
  111.7 0.0 copy-done.5
  111.7 0.1 multiply_add_fusion
  111.8 77.6 %all-to-all-done.1 = f32[512,2,384]{2,1,0:T(2,128)S(1)} async-done(((f32[512,2,384]{2,1,0:T(2,128)}), f32[512,2,384]{2,1,0:T(2,128)S(1)}, u32[]{:S(2)}, u32[]{:S(2)}) %all-to-all-start.1) | async-done | bytes 1572896 | tf_op jit(solution)/shard_map/all_to_all | solution.py:51
  189.4 1.2 copy.16
  190.6 2.5 reshape_reshape.3
  193.1 2.4 copy.17
  195.5 2.5 reshape.89
  198.0 0.0 copy-done
  198.0 0.0 copy-start.1
  198.0 1.6 fusion.28
  199.6 0.0 copy-start.6
  199.6 1.5 fusion.26
  201.1 0.0 copy-start.2
  201.1 1.5 fusion.14
  202.6 2.8 fusion.15
  205.4 1.2 copy.20
  206.6 82.9 %all_to_all.28 = f32[3,1,2,256,256]{4,2,0,1,3:T(2,128)S(1)} all-to-all(f32[3,1,2,256,256]{4,2,0,1,3:T(2,128)S(1)} %copy.20), channel_id=1, replica_groups=mesh['modes'=64,'rad'=8] {'rad'}, dimensions={3} | all-to-all | bytes 3145728 | tf_op jit(solution)/shard_map/all_to_all | solution.py:69
  289.5 1.4 copy.38
  (8 shorter events, 0.0 us)
Async XLA Ops:
  0.0 198.0 %copy-start = (f32[256,256]{1,0:T(8,128)S(1)}, f32[256,256]{1,0:T(8,128)}, u32[]{:S(2)}) copy-start(f32[256,256]{1,0:T(8,128)} %param.10) | copy-start | bytes 786436
  3.9 53.6 %all-to-all-start = ((bf16[64,3,16,128]{3,2,1,0:T(8,128)(2,1)}), bf16[64,3,16,128]{3,2,1,0:T(8,128)(2,1)S(1)}, u32[]{:S(2)}, u32[]{:S(2)}) async-start(bf16[64,3,16,128]{3,2,1,0:T(8,128)(2,1)} %bitcast.1), calls=%async_computation | async-start | bytes 1572864 | tf_op jit(solution)/shard_map/all_to_all | solution.py:44
  93.2 18.3 %copy-start.3 = (f32[256]{0:T(256)S(1)}, f32[256]{0:T(256)}, u32[]{:S(2)}) copy-start(f32[256]{0:T(256)} %param.12) | copy-start | bytes 3076
  93.2 18.4 %copy-start.4 = (f32[1,256]{1,0:T(1,128)S(1)}, f32[1,256]{1,0:T(1,128)}, u32[]{:S(2)}) copy-start(f32[1,256]{1,0:T(1,128)} %param.15) | copy-start | bytes 3076
  93.2 18.5 %copy-start.5 = (f32[3]{0:T(128)S(1)}, f32[3]{0:T(128)}, u32[]{:S(2)}) copy-start(f32[3]{0:T(128)} %param.9) | copy-start | bytes 40
  93.2 96.2 %all-to-all-start.1 = ((f32[512,2,384]{2,1,0:T(2,128)}), f32[512,2,384]{2,1,0:T(2,128)S(1)}, u32[]{:S(2)}, u32[]{:S(2)}) async-start(f32[512,2,384]{2,1,0:T(2,128)} %reshape.88), calls=%async_computation.1 | async-start | bytes 3145728 | tf_op jit(solution)/shard_map/all_to_all | solution.py:51
  198.0 1.6 copy-start.1
  199.6 1.5 copy-start.6
  201.1 1.5 copy-start.2
where the time goes:
time: 295 us; the launch traced here: 291 us
  waiting for transfers between devices  97.9 us (33%)
  blocking collectives  82.9 us (28%)
  matrix products  40.3 us (14%)
  starting transfers between devices  34 us (12%)
  other arithmetic  17.8 us (6%)
  local copies, waits for them, and re-layouts  17.7 us (6%)
    all_to_all x1, blocking collectives, per_device(): return lax.all_to_all(out, 'rad', split_axis=3, concat_axis=1, tiled=True)  82.9 us
    all_to_all x1, waiting for transfers between devices, per_device(): lax.all_to_all(spec, ('modes', 'rad'), split_axis=0, concat_axis=0, tiled...  77.6 us
    all_to_all x1, waiting for transfers between devices, per_device(): got = lax.all_to_all(x, 'modes', split_axis=0, concat_axis=0, tiled=True)  20.4 us
    all_to_all x1, starting transfers between devices, per_device(): lax.all_to_all(spec, ('modes', 'rad'), split_axis=0, concat_axis=0, tiled...  18.3 us
    convert_element_type x1, other arithmetic, split_table(): upper = table.astype(jnp.bfloat16)  17.6 us
    dot_general x1, matrix products, per_device(): jnp.dot(lo, got, preferred_element_type=jnp.float32)  16.7 us
    dot_general x1, matrix products, per_device(): jnp.dot(up, got, preferred_element_type=jnp.float32)  16.4 us
    all_to_all x1, starting transfers between devices, per_device(): got = lax.all_to_all(x, 'modes', split_axis=0, concat_axis=0, tiled=True)  15.7 us
  transfers between devices with their start and end apart: 2, of which 2 were waited for; matrix products, arithmetic and copies ran while one was open for 6% of the time, Pallas kernels for 0%

commit v1 on v0

--- a/solution.py
+++ b/solution.py
@@ -5,6 +5,13 @@
 from jax.sharding import PartitionSpec as P
 
 GLOBAL = True
+
+
+def trade_parts(x, mesh_axis, split, join):
+    size = lax.axis_size(mesh_axis)
+    blocks = jnp.stack(jnp.split(x, size, axis=split), axis=0)
+    blocks = lax.all_to_all(blocks, mesh_axis, split_axis=0, concat_axis=0)
+    return jnp.concatenate(blocks, axis=join)
 
 
 def split_table(points, rows):
@@ -66,7 +73,7 @@
     returned = jnp.einsum("ri,fciq->fcrq", radial_backward[0], scaled, precision=hi)
     out = jnp.einsum("zq,fcrq->fcrz", axial_inverse_map, returned, precision=hi)
     out = out.reshape(fields, 1, 2, nr, nz)
-    return lax.all_to_all(out, "rad", split_axis=3, concat_axis=1, tiled=True)
+    return trade_parts(out, "rad", 3, 1)
 
 
 def solution(mesh):

time: 295 us -> 294 us (level)
  no operation moved by 1% of the time
where the time goes in v1:
time: 294 us; the launch traced here: 290 us
  waiting for transfers between devices  98 us (33%)
  blocking collectives  83 us (28%)
  matrix products  40.4 us (14%)
  starting transfers between devices  33.7 us (11%)
  other arithmetic  17.8 us (6%)
  local copies, waits for them, and re-layouts  16.5 us (6%)
    all_to_all x1, blocking collectives, trade_parts(): blocks = lax.all_to_all(blocks, mesh_axis, split_axis=0, concat_axis=0)  83 us
    all_to_all x1, waiting for transfers between devices, per_device(): lax.all_to_all(spec, ('modes', 'rad'), split_axis=0, concat_axis=0, tiled...  77.6 us
    all_to_all x1, waiting for transfers between devices, per_device(): got = lax.all_to_all(x, 'modes', split_axis=0, concat_axis=0, tiled=True)  20.4 us
    all_to_all x1, starting transfers between devices, per_device(): lax.all_to_all(spec, ('modes', 'rad'), split_axis=0, concat_axis=0, tiled...  18 us
    convert_element_type x1, other arithmetic, split_table(): upper = table.astype(jnp.bfloat16)  17.6 us
    dot_general x1, matrix products, per_device(): jnp.dot(up, got, preferred_element_type=jnp.float32)  16.7 us
    dot_general x1, matrix products, per_device(): jnp.dot(lo, got, preferred_element_type=jnp.float32)  16.5 us
    all_to_all x1, starting transfers between devices, per_device(): got = lax.all_to_all(x, 'modes', split_axis=0, concat_axis=0, tiled=True)  15.7 us
  transfers between devices with their start and end apart: 2, of which 2 were waited for; matrix products, arithmetic and copies ran while one was open for 6% of the time, Pallas kernels for 0%

profile of v1, /device:TPU:32, one launch (start us, length us, event | category | flops | bytes accessed | tf_op | source)
XLA Modules:
  0.0 289.8 jit_solution(5988936400104728893)
XLA Ops:
  0.0 0.0 copy-start
  0.0 2.1 reshape.91
  2.1 1.8 copy.14
  3.9 15.7 %all-to-all-start = ((bf16[64,3,16,128]{3,2,1,0:T(8,128)(2,1)}), bf16[64,3,16,128]{3,2,1,0:T(8,128)(2,1)S(1)}, u32[]{:S(2)}, u32[]{:S(2)}) async-start(bf16[64,3,16,128]{3,2,1,0:T(8,128)(2,1)} %bitcast.1), calls=%async_computation | async-start | bytes 1572864 | tf_op jit(solution)/shard_map/all_to_all | solution.py:51
  19.5 17.6 %fusion.11 = bf16[1024,1024]{1,0:T(8,128)(2,1)S(1)} fusion(f32[1024]{0:T(1024)S(1)} %fusion.45, s32[1024]{0:T(1024)S(1)} %add_select_fusion.1), kind=kLoop, calls=%fused_computation.14 | loop fusion | flops 17825792 | bytes 2105344 | tf_op jit(solution)/shard_map/convert_element_type | solution.py:24
  37.1 20.4 %all-to-all-done = bf16[64,3,16,128]{3,2,1,0:T(8,128)(2,1)S(1)} async-done(((bf16[64,3,16,128]{3,2,1,0:T(8,128)(2,1)}), bf16[64,3,16,128]{3,2,1,0:T(8,128)(2,1)S(1)}, u32[]{:S(2)}, u32[]{:S(2)}) %all-to-all-start) | async-done | bytes 786464 | tf_op jit(solution)/shard_map/all_to_all | solution.py:51
  57.5 0.5 copy.15
  58.0 16.5 %fusion.9 = f32[1024,384]{1,0:T(8,128)S(1)} fusion(bf16[1024,1024]{1,0:T(8,128)(2,1)S(1)} %fusion.11, f32[1024]{0:T(1024)S(1)} %fusion.45, s32[1024]{0:T(1024)S(1)} %add_select_fusion.1, bf16[128,8,3,128]{3,2,1,0:T(4,128)(2,1)S(1)} %bitcast.91), kind=kOutput, calls=%fused_computation.13 | convolution fusion | flops 825229312 | bytes 4464640 | tf_op jit(solution)/shard_map/dot_general | solution.py:53
  74.6 16.7 %convolution_add_fusion = f32[1024,384]{1,0:T(8,128)S(1)} fusion(f32[1024,384]{1,0:T(8,128)S(1)} %fusion.9, bf16[128,8,3,128]{3,2,1,0:T(4,128)(2,1)S(1)} %bitcast.92, f32[1024]{0:T(1024)S(1)} %fusion.45, s32[1024]{0:T(1024)S(1)} %add_select_fusion.1), kind=kOutput, calls=%fused_computation.20 | convolution fusion | flops 823525376 | bytes 3940352 | tf_op jit(solution)/shard_map/dot_general | solution.py:53
  91.2 2.1 reshape.94
  93.3 18.0 %all-to-all-start.1 = ((f32[512,2,384]{2,1,0:T(2,128)}), f32[512,2,384]{2,1,0:T(2,128)S(1)}, u32[]{:S(2)}, u32[]{:S(2)}) async-start(f32[512,2,384]{2,1,0:T(2,128)} %reshape.94), calls=%async_computation.1 | async-start | bytes 3145728 | tf_op jit(solution)/shard_map/all_to_all | solution.py:58
  111.3 0.0 copy-done.3
  111.3 0.0 copy-done.4
  111.3 0.1 broadcast_add_fusion
  111.4 0.0 copy-done.5
  111.4 0.1 multiply_add_fusion
  111.6 77.6 %all-to-all-done.1 = f32[512,2,384]{2,1,0:T(2,128)S(1)} async-done(((f32[512,2,384]{2,1,0:T(2,128)}), f32[512,2,384]{2,1,0:T(2,128)S(1)}, u32[]{:S(2)}, u32[]{:S(2)}) %all-to-all-start.1) | async-done | bytes 1572896 | tf_op jit(solution)/shard_map/all_to_all | solution.py:58
  189.2 1.2 copy.16
  190.5 2.5 reshape_reshape.3
  193.0 2.4 copy.17
  195.3 2.5 reshape.95
  197.9 0.0 copy-done
  197.9 0.0 copy-start.1
  197.9 1.6 fusion.28
  199.5 0.0 copy-start.6
  199.5 1.5 fusion.26
  200.9 0.0 copy-done.6
  200.9 0.0 copy-start.2
  201.0 1.5 fusion.14
  202.5 2.7 fusion.15
  205.4 83.0 %all_to_all.15 = f32[8,3,1,2,32,256]{5,4,3,1,2,0:T(8,128)S(1)} all-to-all(f32[8,3,1,2,32,256]{5,4,3,1,2,0:T(8,128)S(1)} %fusion.30), channel_id=1, replica_groups=mesh['modes'=64,'rad'=8] {'rad'}, dimensions={0} | all-to-all | bytes 3145728 | tf_op jit(solution)/shard_map/all_to_all | solution.py:13
  288.4 1.3 copy.20
  (15 shorter events, 0.1 us)
Async XLA Ops:
  0.0 197.9 %copy-start = (f32[256,256]{1,0:T(8,128)S(1)}, f32[256,256]{1,0:T(8,128)}, u32[]{:S(2)}) copy-start(f32[256,256]{1,0:T(8,128)} %param.10) | copy-start | bytes 786436
  3.9 53.6 %all-to-all-start = ((bf16[64,3,16,128]{3,2,1,0:T(8,128)(2,1)}), bf16[64,3,16,128]{3,2,1,0:T(8,128)(2,1)S(1)}, u32[]{:S(2)}, u32[]{:S(2)}) async-start(bf16[64,3,16,128]{3,2,1,0:T(8,128)(2,1)} %bitcast.1), calls=%async_computation | async-start | bytes 1572864 | tf_op jit(solution)/shard_map/all_to_all | solution.py:51
  93.3 18.0 %copy-start.3 = (f32[256]{0:T(256)S(1)}, f32[256]{0:T(256)}, u32[]{:S(2)}) copy-start(f32[256]{0:T(256)} %param.12) | copy-start | bytes 3076
  93.3 18.0 %copy-start.4 = (f32[1,256]{1,0:T(1,128)S(1)}, f32[1,256]{1,0:T(1,128)}, u32[]{:S(2)}) copy-start(f32[1,256]{1,0:T(1,128)} %param.15) | copy-start | bytes 3076
  93.3 18.1 %copy-start.5 = (f32[3]{0:T(128)S(1)}, f32[3]{0:T(128)}, u32[]{:S(2)}) copy-start(f32[3]{0:T(128)} %param.9) | copy-start | bytes 40
  93.3 95.9 %all-to-all-start.1 = ((f32[512,2,384]{2,1,0:T(2,128)}), f32[512,2,384]{2,1,0:T(2,128)S(1)}, u32[]{:S(2)}, u32[]{:S(2)}) async-start(f32[512,2,384]{2,1,0:T(2,128)} %reshape.94), calls=%async_computation.1 | async-start | bytes 3145728 | tf_op jit(solution)/shard_map/all_to_all | solution.py:58
  197.9 1.6 copy-start.1
  199.5 1.5 copy-start.6
  200.9 1.5 copy-start.2
